TPU v7x, 32 devices: a whole 2x2x4 slice. The times are simulated.
32 devices in a mesh: row: 4 (over y, x), col: 4 (over z), dp: 2 (over core).
Axes of the slice: x: 2, y: 2, z: 4, core: 2. Of those that a mesh axis runs over, the one named last changes fastest.
Arguments:
- tokens: bfloat16 [512, 8192], P(('row', 'dp'), 'col'), may hold values from -6 to 6
- upstream: bfloat16 [512, 8192], P(('row', 'dp'), 'col'), may hold values from -1.5 to 1.5
- w_gate: bfloat16 [8192, 14336], P('col', 'row'), may hold values from -0.0625 to 0.0625
- w_up: bfloat16 [8192, 14336], P('col', 'row'), may hold values from -0.0625 to 0.0625
- w_down: bfloat16 [14336, 8192], P('row', 'col'), may hold values from -0.046875 to 0.046875
- delta_gate: bfloat16 [4, 4, 192, 128, 128], P('col', 'row'), may hold values from -0.03125 to 0.03125
- delta_up: bfloat16 [4, 4, 192, 128, 128], P('col', 'row'), may hold values from -0.03125 to 0.03125
- delta_down: bfloat16 [4, 4, 192, 128, 128], P('row', 'col'), may hold values from -0.0234375 to 0.0234375
- pattern_gate: int32 [4, 4, 192], P('col', 'row'), may hold values from 0 to 448, as said below
- pattern_up: int32 [4, 4, 192], P('col', 'row'), may hold values from 0 to 448, as said below
- pattern_down: int32 [4, 4, 192], P('row', 'col'), may hold values from 0 to 448, as said below
Outputs:
- output: bfloat16 [512, 8192], P(('row', 'dp'), 'col')
- input_grad: bfloat16 [512, 8192], P(('row', 'dp'), 'col')
- delta_grad_gate: float32 [4, 4, 192, 128, 128], P('col', 'row', 'dp')
- delta_grad_up: float32 [4, 4, 192, 128, 128], P('col', 'row', 'dp')
- delta_grad_down: float32 [4, 4, 192, 128, 128], P('row', 'col', 'dp')
Inputs may be any that keep to these rules, and one draw needn't show every extreme that they name: `pattern_gate`: in each tile the 192 slots name distinct blocks of that tile; the value 448 marks an empty slot; live slots come first, a tile holds 48 to 192 of them, and some tile holds 192. `pattern_up`: as for pattern_gate. `pattern_down`: as for pattern_gate.
All inputs are finite; a program needn't handle non-finite values.
Results may differ from a plain program's by a relative error of at most 0.0058.
Values may be sent and summed in bfloat16 or wider, within the bound.
A program may use at most 320 MiB of HBM per device.

v0:
```python
import jax
import jax.numpy as jnp
from jax import lax
from jax.sharding import PartitionSpec as P


def fold_tile(weight, blocks, pattern):
    block_size = blocks.shape[-1]
    row_blocks = weight.shape[0] // block_size
    column_blocks = weight.shape[1] // block_size
    slot_list = pattern.reshape(-1)
    flat_blocks = blocks.reshape(slot_list.shape[0], block_size, block_size)
    numbers = jnp.arange(row_blocks * column_blocks, dtype=jnp.int32)
    one_hot = (slot_list[:, None] == numbers[None, :]).astype(jnp.bfloat16)
    placed = jnp.einsum("sk,sij->kij", one_hot, flat_blocks, preferred_element_type=jnp.float32)
    placed = placed.reshape(row_blocks, column_blocks, block_size, block_size)
    placed = placed.transpose(0, 2, 1, 3).reshape(weight.shape)
    return (weight.astype(jnp.float32) + placed).astype(jnp.bfloat16)


def tile_grads(left_rows, right_rows, slot_list, block_size):
    left_count = left_rows.shape[1] // block_size
    right_count = right_rows.shape[1] // block_size
    tile_blocks = left_count * right_count
    usable = (slot_list < tile_blocks).astype(jnp.float32)
    clipped = jnp.minimum(slot_list, tile_blocks - 1)
    left_pick = jnp.take(
        left_rows.reshape(left_rows.shape[0], left_count, block_size),
        clipped // right_count,
        axis=1,
    )
    right_pick = jnp.take(
        right_rows.reshape(right_rows.shape[0], right_count, block_size),
        clipped % right_count,
        axis=1,
    )
    result = jnp.einsum("tsi,tsj->sij", left_pick, right_pick, preferred_element_type=jnp.float32)
    return result * usable[:, None, None]


def dot_transposed(left_rows, right_rows):
    return lax.dot_general(
        left_rows, right_rows, (((1,), (1,)), ((), ())), preferred_element_type=jnp.float32
    )


def local(
    tokens,
    upstream,
    w_gate,
    w_up,
    w_down,
    delta_gate,
    delta_up,
    delta_down,
    pattern_gate,
    pattern_up,
    pattern_down,
):
    block_size = delta_gate.shape[-1]
    gate_folded = fold_tile(w_gate, delta_gate, pattern_gate)
    up_folded = fold_tile(w_up, delta_up, pattern_up)
    down_folded = fold_tile(w_down, delta_down, pattern_down)
    hidden_width = gate_folded.shape[1]
    joined = jnp.concatenate((gate_folded, up_folded), axis=1)
    token_all, upstream_all = (
        lax.all_gather(tokens, "row", axis=0, tiled=True),
        lax.all_gather(upstream, "row", axis=0, tiled=True),
    )
    row_block = token_all
    totals = lax.psum_scatter(
        jnp.dot(row_block, joined, preferred_element_type=jnp.float32),
        "col",
        scatter_dimension=0,
        tiled=True,
    )
    gate_mine = totals[:, :hidden_width]
    up_mine = totals[:, hidden_width:]
    hidden_mine = (gate_mine * jax.nn.sigmoid(gate_mine) * up_mine).astype(jnp.bfloat16)
    hidden_all = lax.all_gather(hidden_mine, "col", axis=0, tiled=True)
    row_block = hidden_all
    output = lax.psum_scatter(
        jnp.dot(row_block, down_folded, preferred_element_type=jnp.float32),
        "row",
        scatter_dimension=0,
        tiled=True,
    ).astype(jnp.bfloat16)
    row_block = upstream_all
    backward_mine = lax.psum_scatter(
        dot_transposed(row_block, down_folded), "col", scatter_dimension=0, tiled=True
    )
    sigmoid_mine = jax.nn.sigmoid(gate_mine)
    grad_gate = (
        backward_mine * up_mine * sigmoid_mine * (1.0 + gate_mine * (1.0 - sigmoid_mine))
    ).astype(jnp.bfloat16)
    grad_up = (backward_mine * gate_mine * sigmoid_mine).astype(jnp.bfloat16)
    grads_joined = lax.all_gather(
        jnp.concatenate((grad_gate, grad_up), axis=1), "col", axis=0, tiled=True
    )
    row_block = grads_joined
    input_grad = lax.psum_scatter(
        dot_transposed(row_block, joined), "row", scatter_dimension=0, tiled=True
    ).astype(jnp.bfloat16)
    grad_terms = (
        tile_grads(token_all, grads_joined[:, :hidden_width], pattern_gate.reshape(-1), block_size),
        tile_grads(token_all, grads_joined[:, hidden_width:], pattern_up.reshape(-1), block_size),
        tile_grads(hidden_all, upstream_all, pattern_down.reshape(-1), block_size),
    )
    grad_gate_mine, grad_up_mine, grad_down_mine = (
        lax.psum_scatter(grad_terms[0], "dp", scatter_dimension=0, tiled=True),
        lax.psum_scatter(grad_terms[1], "dp", scatter_dimension=0, tiled=True),
        lax.psum_scatter(grad_terms[2], "dp", scatter_dimension=0, tiled=True),
    )
    delta_grad_gate = grad_gate_mine.reshape((1, 1) + grad_gate_mine.shape)
    delta_grad_up = grad_up_mine.reshape((1, 1) + grad_up_mine.shape)
    delta_grad_down = grad_down_mine.reshape((1, 1) + grad_down_mine.shape)
    return (output, input_grad, delta_grad_gate, delta_grad_up, delta_grad_down)


def solution(mesh):
    return jax.shard_map(
        local,
        mesh=mesh,
        in_specs=(
            P(("row", "dp"), "col"),
            P(("row", "dp"), "col"),
            P("col", "row"),
            P("col", "row"),
            P("row", "col"),
            P("col", "row", None, None, None),
            P("col", "row", None, None, None),
            P("row", "col", None, None, None),
            P("col", "row", None),
            P("col", "row", None),
            P("row", "col", None),
        ),
        out_specs=(
            P(("row", "dp"), "col"),
            P(("row", "dp"), "col"),
            P("col", "row", "dp", None, None),
            P("col", "row", "dp", None, None),
            P("row", "col", "dp", None, None),
        ),
        check_vma=False,
    )
```

profile of v0, /device:TPU:1, one launch (start us, length us, event | category | flops | bytes accessed | tf_op | source)
XLA Modules:
  0.0 742.4 jit_solution(11663043650277400420)
XLA Ops:
  8.7 18.7 %fusion.29 = f32[16,28,128,128]{3,1,2,0:T(8,128)} fusion(bf16[192,128,128]{2,1,0:T(8,128)(2,1)} %bitcast.108, s32[16,28]{1,0:T(8,128)S(1)} %multiply_add_fusion.1, s32[192]{0:T(256)} %bitcast.117), kind=kOutput, calls=%fused_computation.41 | convolution fusion | flops 2818658304 | bytes 35654144 | tf_op jit(solution)/shard_map/sk,sij->kij/dot_general | solution.py:15
  27.5 19.3 %fusion.25 = f32[28,16,128,128]{3,1,2,0:T(8,128)} fusion(bf16[192,128,128]{2,1,0:T(8,128)(2,1)S(1)} %bitcast.111, s32[28,16]{1,0:T(8,128)S(1)} %multiply_add_fusion, s32[192]{0:T(256)S(1)} %bitcast.115), kind=kOutput, calls=%fused_computation.37 | convolution fusion | flops 2818658304 | bytes 35654144 | tf_op jit(solution)/shard_map/sk,sij->kij/dot_general | solution.py:15
  46.7 24.8 %convolution_bitcast_fusion = f32[256,3584]{0,1:T(8,128)} fusion(bf16[256,2048]{1,0:T(8,128)(2,1)} %all-gather.9.cloned.1.call-done, f32[448,8,16,128]{3,2,1,0:T(8,128)} %bitcast.99, bf16[3584,2048]{1,0:T(8,128)(2,1)} %param.19), kind=kOutput, calls=%fused_computation.52 | convolution fusion | flops 3780116480 | bytes 48758784 | tf_op jit(solution)/shard_map/dot_general | solution.py:42
  71.6 5.1 copy.120
  76.8 19.0 %fusion.27 = f32[16,28,128,128]{3,1,2,0:T(8,128)} fusion(bf16[192,128,128]{2,1,0:T(8,128)(2,1)} %bitcast.112, s32[192]{0:T(256)S(1)} %bitcast.119, s32[16,28]{1,0:T(8,128)S(1)} %multiply_add_fusion.1), kind=kOutput, calls=%fused_computation.39 | convolution fusion | flops 2818658304 | bytes 35654144 | tf_op jit(solution)/shard_map/sk,sij->kij/dot_general | solution.py:15
  95.8 34.6 %copy.145 = f32[256,8,28,128]{3,1,2,0:T(8,128)} copy(f32[256,8,28,128]{3,2,1,0:T(8,128)} %bitcast.101) | data formatting | bytes 58720256
  130.4 29.8 %copy.116 = f32[2048,3584]{0,1:T(8,128)} copy(f32[2048,3584]{1,0:T(8,128)} %bitcast.103) | data formatting | bytes 58720256 | tf_op jit(solution)/shard_map/reshape | solution.py:17
  160.2 34.7 %copy.144 = f32[256,8,28,128]{3,1,2,0:T(8,128)} copy(f32[256,8,28,128]{3,2,1,0:T(8,128)} %bitcast.102) | data formatting | bytes 58720256
  194.9 29.7 %copy.117 = f32[2048,3584]{0,1:T(8,128)} copy(f32[2048,3584]{1,0:T(8,128)} %bitcast.104) | data formatting | bytes 58720256 | tf_op jit(solution)/shard_map/reshape | solution.py:17
  224.6 20.4 %copy.85 = bf16[2048,3584]{0,1:T(8,128)(2,1)} copy(bf16[2048,3584]{1,0:T(8,128)(2,1)} %param.17) | data formatting | bytes 29360128 | tf_op args[2]
  244.9 20.4 %copy.88 = bf16[2048,3584]{0,1:T(8,128)(2,1)} copy(bf16[2048,3584]{1,0:T(8,128)(2,1)} %param.18) | data formatting | bytes 29360128 | tf_op args[3]
  265.3 39.0 %add_convert_fusion = (bf16[2048,3584]{0,1:T(8,128)(2,1)}, bf16[2048,3584]{0,1:T(8,128)(2,1)}) fusion(f32[2048,3584]{0,1:T(8,128)} %copy.117, bf16[2048,3584]{0,1:T(8,128)(2,1)} %copy.88, f32[2048,3584]{0,1:T(8,128)} %copy.116, bf16[2048,3584]{0,1:T(8,128)(2,1)} %copy.85), kind=kLoop, calls=%fused_computation.11 | loop fusion | flops 44040192 | bytes 117440512 | tf_op jit(solution)/shard_map/convert_element_type | solution.py:18
  304.4 16.0 %fusion.24 = f32[256,7168]{0,1:T(8,128)} fusion(bf16[256,2048]{1,0:T(8,128)(2,1)} %all-gather.5.cloned.1.call-done, bf16[2048,3584]{0,1:T(8,128)(2,1)} %get-tuple-element.33, bf16[2048,3584]{0,1:T(8,128)(2,1)} %get-tuple-element.34), kind=kOutput, calls=%fused_computation.36 | convolution fusion | flops 7574913024 | bytes 37748736 | tf_op jit(solution)/shard_map/dot_general | solution.py:72
  320.3 8.4 %copy.118 = f32[256,7168]{1,0:T(8,128)} copy(f32[256,7168]{0,1:T(8,128)} %fusion.24) | data formatting | bytes 14680064
  328.9 129.6 %reduce-scatter.22.cloned.1.call-done = f32[64,7168]{1,0:T(8,128)} async-done(((f32[256,7168]{1,0:T(8,128)}), f32[64,7168]{1,0:T(8,128)}) %reduce-scatter.22.cloned.1.call-update) | async-done | bytes 1835024 | tf_op jit(solution)/shard_map/reduce_scatter | solution.py:71
  458.5 3.0 multiply_convert_fusion.1
  462.6 40.7 %all-gather.7.cloned.1.call-done = bf16[256,3584]{1,0:T(8,128)(2,1)} async-done(((bf16[64,3584]{1,0:T(8,128)(2,1)}), bf16[256,3584]{1,0:T(8,128)(2,1)}) %all-gather.7.cloned.1.call-update) | async-done | bytes 1835024 | tf_op jit(solution)/shard_map/all_gather | solution.py:80
  503.3 22.8 %fusion.67 = f32[256,2048]{1,0:T(8,128)} fusion(bf16[256,3584]{1,0:T(8,128)(2,1)} %all-gather.7.cloned.1.call-done, f32[448,8,16,128]{3,2,1,0:T(8,128)} %bitcast.100, bf16[3584,2048]{1,0:T(8,128)(2,1)} %param.19), kind=kOutput, calls=%fused_computation.111 | convolution fusion | flops 3780116480 | bytes 47972352 | tf_op jit(solution)/shard_map/dot_general | solution.py:83
  526.1 50.2 %all-gather.11.cloned.1.call-done = bf16[256,7168]{1,0:T(8,128)(2,1)} async-done(((bf16[64,7168]{1,0:T(8,128)(2,1)}), bf16[256,7168]{1,0:T(8,128)(2,1)}) %all-gather.11.cloned.1.call-update) | async-done | bytes 3670032 | tf_op jit(solution)/shard_map/all_gather | solution.py:97
  576.4 15.2 %fusion.1 = f32[256,2048]{1,0:T(8,128)} fusion(bf16[256,7168]{1,0:T(8,128)(2,1)} %all-gather.11.cloned.1.call-done, bf16[2048,3584]{0,1:T(8,128)(2,1)} %get-tuple-element.33, bf16[2048,3584]{0,1:T(8,128)(2,1)} %get-tuple-element.34), kind=kOutput, calls=%fused_computation.13 | convolution fusion | flops 7574913024 | bytes 35127296 | tf_op jit(solution)/shard_map/dot_general | solution.py:42
  593.4 8.2 %gather_fusion.5 = bf16[192,256,128]{2,1,0:T(8,128)(2,1)} fusion(bf16[256,16,128]{2,0,1:T(8,128)(2,1)S(1)} %copy.108, s32[1024]{0:T(1024)S(1)} %get-tuple-element.39), kind=kCustom, calls=%fused_computation.3.clone | custom fusion | bytes 25166592 | tf_op jit(solution)/shard_map/jit(_take)/gather | solution.py:32
  606.7 8.3 %gather_fusion.4 = bf16[192,256,128]{2,1,0:T(8,128)(2,1)} fusion(bf16[256,28,128]{2,0,1:T(8,128)(2,1)S(1)} %copy.106, s32[1024]{0:T(1024)S(1)} %get-tuple-element.40), kind=kCustom, calls=%fused_computation.5.clone | custom fusion | bytes 25166592 | tf_op jit(solution)/shard_map/jit(_take)/gather | solution.py:27
  615.0 13.9 %broadcast_multiply_fusion = f32[192,128,128]{2,1,0:T(8,128)} fusion(f32[192]{0:T(256)S(1)} %get-tuple-element.26, bf16[192,256,128]{2,1,0:T(8,128)(2,1)} %gather_fusion.5, pred[192]{0:T(512)(128)(4,1)S(1)} %get-tuple-element.24, bf16[192,256,128]{2,1,0:T(8,128)(2,1)} %gather_fusion.4, pred[192]{0:T(512)(128)(4,1)S(1)} %get-tuple-element.7), kind=kOutput, calls=%fused_computation.49 | convolution fusion | flops 1626341376 | bytes 37749888 | tf_op jit(solution)/shard_map/tsi,tsj->sij/dot_general | solution.py:37
  631.5 8.0 %gather_fusion = bf16[192,256,128]{2,1,0:T(8,128)(2,1)} fusion(bf16[256,16,128]{2,0,1:T(8,128)(2,1)S(1)} %copy.97, s32[1024]{0:T(1024)S(1)} %get-tuple-element.36), kind=kCustom, calls=%fused_computation.clone | custom fusion | bytes 25166592 | tf_op jit(solution)/shard_map/jit(_take)/gather | solution.py:27
  639.5 3.5 fusion.69
  648.1 7.9 %gather_fusion.1 = bf16[192,256,128]{2,1,0:T(8,128)(2,1)} fusion(bf16[256,28,128]{2,0,1:T(8,128)(2,1)S(1)} %copy.99, s32[1024]{0:T(1024)S(1)} %get-tuple-element.35), kind=kCustom, calls=%fused_computation.1.clone | custom fusion | bytes 25166592 | tf_op jit(solution)/shard_map/jit(_take)/gather | solution.py:32
  656.0 18.6 %broadcast_multiply_fusion.2 = f32[192,128,128]{2,1,0:T(8,128)} fusion(f32[192]{0:T(256)S(1)} %get-tuple-element.32, bf16[192,256,128]{2,1,0:T(8,128)(2,1)} %gather_fusion.1, pred[192]{0:T(512)(128)(4,1)S(1)} %get-tuple-element.30, bf16[192,256,128]{2,1,0:T(8,128)(2,1)} %gather_fusion, pred[192]{0:T(512)(128)(4,1)S(1)} %get-tuple-element.15), kind=kOutput, calls=%fused_computation.51 | convolution fusion | flops 1626341376 | bytes 37749888 | tf_op jit(solution)/shard_map/tsi,tsj->sij/dot_general | solution.py:37
  675.3 8.1 %gather_fusion.2 = bf16[192,256,128]{2,1,0:T(8,128)(2,1)} fusion(bf16[256,16,128]{2,0,1:T(8,128)(2,1)S(1)} %copy.97, s32[1024]{0:T(1024)S(1)} %get-tuple-element.38), kind=kCustom, calls=%fused_computation.2.clone | custom fusion | bytes 25166592 | tf_op jit(solution)/shard_map/jit(_take)/gather | solution.py:27
  685.7 3.1 copy.103
  688.7 10.4 %gather_fusion.3 = bf16[192,256,128]{2,1,0:T(8,128)(2,1)} fusion(bf16[256,28,128]{2,0,1:T(8,128)(2,1)S(1)} %copy.103, s32[1024]{0:T(1024)S(1)} %get-tuple-element.37), kind=kCustom, calls=%fused_computation.4.clone | custom fusion | bytes 25166592 | tf_op jit(solution)/shard_map/jit(_take)/gather | solution.py:32
  699.1 14.6 %broadcast_multiply_fusion.1 = f32[192,128,128]{2,1,0:T(8,128)} fusion(f32[192]{0:T(256)S(1)} %get-tuple-element.29, bf16[192,256,128]{2,1,0:T(8,128)(2,1)} %gather_fusion.3, pred[192]{0:T(512)(128)(4,1)S(1)} %get-tuple-element.27, bf16[192,256,128]{2,1,0:T(8,128)(2,1)} %gather_fusion.2, pred[192]{0:T(512)(128)(4,1)S(1)} %get-tuple-element.11), kind=kOutput, calls=%fused_computation.50 | convolution fusion | flops 1626341376 | bytes 37749888 | tf_op jit(solution)/shard_map/tsi,tsj->sij/dot_general | solution.py:37
  717.3 18.3 %reduce-scatter.18.cloned.1.call-done = f32[96,128,128]{2,1,0:T(8,128)} async-done(((f32[192,128,128]{2,1,0:T(8,128)}), f32[96,128,128]{2,1,0:T(8,128)}) %reduce-scatter.18.cloned.1.call-update) | async-done | bytes 6291472 | tf_op jit(solution)/shard_map/reduce_scatter | solution.py:111
  (72 shorter events, 24.0 us)
Async XLA Ops:
  7.2 39.6 %all-gather.9.cloned.1.call-start = ((), (), s32[]{:S(2)}) async-start(), calls=%async_computation.10 | async-start | bytes 1310720 | tf_op jit(solution)/shard_map/all_gather | solution.py:68
  7.2 20.2 %slice-start = ((s8[6291456]{0:T(1024)(128)(4,1)}), s8[2097152]{0:T(1024)(128)(4,1)S(1)}, s32[]{:S(2)}) async-start(s8[6291456]{0:T(1024)(128)(4,1)} %bitcast.109), calls=%async_computation.18 | async-start | bytes 4194304
  7.9 296.5 %all-gather.5.cloned.1.call-start = ((), (), s32[]{:S(2)}) async-start(), calls=%async_computation.7 | async-start | bytes 1310720 | tf_op jit(solution)/shard_map/all_gather | solution.py:67
  8.6 320.2 %reduce-scatter.24.cloned.1.call-start = ((), (), s32[]{:S(2)}) async-start(), calls=%async_computation.17 | async-start | bytes 4587520 | tf_op jit(solution)/shard_map/reduce_scatter | solution.py:89
  8.7 18.7 %slice-start.1 = ((s8[6291456]{0:T(1024)(128)(4,1)}), s8[4194304]{0:T(1024)(128)(4,1)S(1)}, s32[]{:S(2)}) async-start(s8[6291456]{0:T(1024)(128)(4,1)} %bitcast.109), calls=%async_computation.19 | async-start | bytes 8388608
  8.7 18.7 %copy-start.4 = (s32[1,1,192]{2,1,0:T(1,128)S(1)}, s32[1,1,192]{2,1,0:T(1,128)}, u32[]{:S(2)}) copy-start(s32[1,1,192]{2,1,0:T(1,128)} %param.25) | copy-start | bytes 2308
  46.7 30.0 %copy-start.7 = (s32[1,1,192]{2,1,0:T(1,128)S(1)}, s32[1,1,192]{2,1,0:T(1,128)}, u32[]{:S(2)}) copy-start(s32[1,1,192]{2,1,0:T(1,128)} %param.24) | copy-start | bytes 2308
  76.7 381.8 %reduce-scatter.22.cloned.1.call-start = ((), (), s32[]{:S(2)}) async-start(), calls=%async_computation.16 | async-start | bytes 9175040 | tf_op jit(solution)/shard_map/reduce_scatter | solution.py:71
  328.8 174.5 %all-gather.7.cloned.1.call-start = ((), (), s32[]{:S(2)}) async-start(), calls=%async_computation.8 | async-start | bytes 2293760 | tf_op jit(solution)/shard_map/all_gather | solution.py:80
  461.5 114.9 %all-gather.11.cloned.1.call-start = ((), (), s32[]{:S(2)}) async-start(), calls=%async_computation.11 | async-start | bytes 4587520 | tf_op jit(solution)/shard_map/all_gather | solution.py:97
  462.6 251.2 %reduce-scatter.12.cloned.1.call-start = ((), (), s32[]{:S(2)}) async-start(), calls=%async_computation.9 | async-start | bytes 2621440 | tf_op jit(solution)/shard_map/reduce_scatter | solution.py:82
  526.1 65.6 %copy-start.5 = (s32[1,1,192]{2,1,0:T(1,128)S(1)}, s32[1,1,192]{2,1,0:T(1,128)}, u32[]{:S(2)}) copy-start(s32[1,1,192]{2,1,0:T(1,128)} %param.25) | copy-start | bytes 2308
  526.1 65.6 %copy-start.2 = (bf16[256,2048]{1,0:T(8,128)(2,1)S(1)}, bf16[256,2048]{1,0:T(8,128)(2,1)}, u32[]{:S(2)}) copy-start(bf16[256,2048]{1,0:T(8,128)(2,1)} %all-gather.9.cloned.1.call-done) | copy-start | bytes 3145732
  526.1 189.5 %reduce-scatter.14.cloned.1.call-start = ((), (), s32[]{:S(2)}) async-start(), calls=%async_computation.12 | async-start | bytes 2621440 | tf_op jit(solution)/shard_map/reduce_scatter | solution.py:101
  591.6 125.7 %reduce-scatter.20.cloned.1.call-start = ((), (), s32[]{:S(2)}) async-start(), calls=%async_computation.15 | async-start | bytes 18874368 | tf_op jit(solution)/shard_map/reduce_scatter | solution.py:112
  593.3 8.2 %copy-start.1 = (bf16[256,3584]{1,0:T(8,128)(2,1)S(1)}, bf16[256,3584]{1,0:T(8,128)(2,1)}, u32[]{:S(2)}) copy-start(bf16[256,3584]{1,0:T(8,128)(2,1)} %all-gather.7.cloned.1.call-done) | copy-start | bytes 5505028
  628.9 0.7 copy-start.6
  628.9 1.2 copy-start.3
  628.9 88.4 %reduce-scatter.16.cloned.1.call-start = ((), (), s32[]{:S(2)}) async-start(), calls=%async_computation.13 | async-start | bytes 18874368 | tf_op jit(solution)/shard_map/reduce_scatter | solution.py:110
  674.6 0.7 copy-start.8
  674.6 61.0 %reduce-scatter.18.cloned.1.call-start = ((), (), s32[]{:S(2)}) async-start(), calls=%async_computation.14 | async-start | bytes 18874368 | tf_op jit(solution)/shard_map/reduce_scatter | solution.py:111
  675.3 8.1 %copy-start = (bf16[256,3584]{1,0:T(8,128)(2,1)S(1)}, bf16[256,3584]{1,0:T(8,128)(2,1)}, u32[]{:S(2)}) copy-start(bf16[256,3584]{1,0:T(8,128)(2,1)} %get-tuple-element.19) | copy-start | bytes 5505028
Sparse Core Ops, SparseCore 0:
  9.8 28.3 all-gather.8
  40.1 26.4 all-gather.4
  76.8 70.0 reduce-scatter.23
  328.9 129.5 reduce-scatter.21
  461.6 41.6 all-gather.6
  505.3 71.0 all-gather.10
  579.3 33.7 reduce-scatter.11
  616.0 35.1 reduce-scatter.13
  654.2 22.4 reduce-scatter.19
  679.4 23.1 reduce-scatter.15
  713.9 21.7 reduce-scatter.17
where the time goes:
time: 753 us; the launch traced here: 742 us
  local copies, waits for them, and re-layouts  258 us (34%)
  waiting for transfers between devices  240 us (32%)
  matrix products  183 us (24%)
  other arithmetic  46.7 us (6%)
  between operations  14.3 us (2%)
    unnamed x30, local copies, waits for them, and re-layouts  130 us
    reduce_scatter x1, waiting for transfers between devices, local(): lax.psum_scatter(jnp.dot(row_block, joined, preferred_element_type=jnp.fl...  130 us
    reshape x2, local copies, waits for them, and re-layouts, fold_tile(): placed = placed.transpose(0, 2, 1, 3).reshape(weight.shape)  59.5 us
    dot_general x3, matrix products, fold_tile(): jnp.einsum('sk,sij->kij', one_hot, flat_blocks, preferred_element_type=jn...  57 us
    all_gather x1, waiting for transfers between devices, local(): lax.all_gather(jnp.concatenate((grad_gate, grad_up), axis=1), 'col', axis...  50.2 us
    dot_general x3, matrix products, tile_grads(): jnp.einsum('tsi,tsj->sij', left_pick, right_pick, preferred_element_type=...  47 us
    all_gather x1, waiting for transfers between devices, local(): hidden_all = lax.all_gather(hidden_mine, 'col', axis=0, tiled=True)  40.7 us
    dot_general x2, matrix products, dot_transposed(): lax.dot_general(left_rows, right_rows, (((1,), (1,)), ((), ())), preferre...  40 us
  transfers between devices with their start and end apart: 11, of which 4 were waited for; matrix products, arithmetic and copies ran while one was open for 65% of the time, Pallas kernels for 0%

commit v1 on v0

--- a/solution.py
+++ b/solution.py
@@ -2,6 +2,16 @@
 import jax.numpy as jnp
 from jax import lax
 from jax.sharding import PartitionSpec as P
+
+
+def turned_line(x, axis, d):
+    devices = lax.axis_size(axis)
+    current, blocks = (x, [x])
+    for _ in range(devices - 1):
+        current = lax.ppermute(current, axis, [(i, (i + 1) % devices) for i in range(devices)])
+        blocks.insert(0, current)
+    flat = jnp.concatenate(blocks, axis=d)
+    return jnp.roll(flat, (lax.axis_index(axis) + 1) * x.shape[d], axis=d)
 
 
 def fold_tile(weight, blocks, pattern):
@@ -77,7 +87,7 @@
     gate_mine = totals[:, :hidden_width]
     up_mine = totals[:, hidden_width:]
     hidden_mine = (gate_mine * jax.nn.sigmoid(gate_mine) * up_mine).astype(jnp.bfloat16)
-    hidden_all = lax.all_gather(hidden_mine, "col", axis=0, tiled=True)
+    hidden_all = turned_line(hidden_mine, "col", 0)
     row_block = hidden_all
     output = lax.psum_scatter(
         jnp.dot(row_block, down_folded, preferred_element_type=jnp.float32),

time: 753 us -> 742 us (0.985)
  waiting for transfers between devices: 240 us -> 226 us
    all_gather x1 -> x0, waiting for transfers between devices: 40.7 us -> none  [local(): hidden_all = lax.all_gather(hidden_mine, 'col', axis=0, tiled=True)]
    ppermute x0 -> x3, waiting for transfers between devices: none -> 34.6 us  [turned_line(): lax.ppermute(current, axis, [(i, (i + 1) % devices) for i in range(device...]
    all_gather x1, waiting for transfers between devices: 50.2 us -> 42.3 us  [local(): lax.all_gather(jnp.concatenate((grad_gate, grad_up), axis=1), 'col', axis...]
    unnamed x30 -> x35, local copies, waits for them, and re-layouts: 130 us -> 130 us
  transfers between devices with their start and end apart: 11 -> 13, of which waited for: 4 -> 6; matrix products, arithmetic and copies ran while one was open for 65% -> 66% of each run, Pallas kernels for 0% -> 0%
where the time goes in v1:
time: 742 us; the launch traced here: 731 us
  local copies, waits for them, and re-layouts  259 us (35%)
  waiting for transfers between devices  226 us (30%)
  matrix products  184 us (25%)
  other arithmetic  45.9 us (6%)
  between operations  14.7 us (2%)
    unnamed x35, local copies, waits for them, and re-layouts  130 us
    reduce_scatter x1, waiting for transfers between devices, local(): lax.psum_scatter(jnp.dot(row_block, joined, preferred_element_type=jnp.fl...  130 us
    reshape x2, local copies, waits for them, and re-layouts, fold_tile(): placed = placed.transpose(0, 2, 1, 3).reshape(weight.shape)  59.4 us
    dot_general x3, matrix products, fold_tile(): jnp.einsum('sk,sij->kij', one_hot, flat_blocks, preferred_element_type=jn...  57 us
    dot_general x3, matrix products, tile_grads(): jnp.einsum('tsi,tsj->sij', left_pick, right_pick, preferred_element_type=...  48.6 us
    all_gather x1, waiting for transfers between devices, local(): lax.all_gather(jnp.concatenate((grad_gate, grad_up), axis=1), 'col', axis...  42.3 us
    dot_general x2, matrix products, dot_transposed(): lax.dot_general(left_rows, right_rows, (((1,), (1,)), ((), ())), preferre...  40.1 us
    convert_element_type x1, other arithmetic, fold_tile(): return (weight.astype(jnp.float32) + placed).astype(jnp.bfloat16)  39 us
  transfers between devices with their start and end apart: 13, of which 6 were waited for; matrix products, arithmetic and copies ran while one was open for 66% of the time, Pallas kernels for 0%

profile of v1, /device:TPU:1, one launch (start us, length us, event | category | flops | bytes accessed | tf_op | source)
XLA Modules:
  0.0 730.8 jit_solution(706147929298305518)
XLA Ops:
  8.7 18.7 %fusion.29 = f32[16,28,128,128]{3,1,2,0:T(8,128)} fusion(bf16[192,128,128]{2,1,0:T(8,128)(2,1)} %bitcast.108, s32[16,28]{1,0:T(8,128)S(1)} %multiply_add_fusion.1, s32[192]{0:T(256)} %bitcast.117), kind=kOutput, calls=%fused_computation.41 | convolution fusion | flops 2818658304 | bytes 35654144 | tf_op jit(solution)/shard_map/sk,sij->kij/dot_general | solution.py:25
  27.5 19.3 %fusion.25 = f32[28,16,128,128]{3,1,2,0:T(8,128)} fusion(bf16[192,128,128]{2,1,0:T(8,128)(2,1)S(1)} %bitcast.111, s32[28,16]{1,0:T(8,128)S(1)} %multiply_add_fusion, s32[192]{0:T(256)S(1)} %bitcast.115), kind=kOutput, calls=%fused_computation.37 | convolution fusion | flops 2818658304 | bytes 35654144 | tf_op jit(solution)/shard_map/sk,sij->kij/dot_general | solution.py:25
  46.7 24.8 %convolution_bitcast_fusion = f32[256,3584]{0,1:T(8,128)} fusion(bf16[256,2048]{1,0:T(8,128)(2,1)} %all-gather.6.cloned.1.call-done, f32[448,8,16,128]{3,2,1,0:T(8,128)} %bitcast.99, bf16[3584,2048]{1,0:T(8,128)(2,1)} %param.19), kind=kOutput, calls=%fused_computation.52 | convolution fusion | flops 3780116480 | bytes 48758784 | tf_op jit(solution)/shard_map/dot_general | solution.py:52
  71.6 5.1 copy.151
  76.8 19.0 %fusion.27 = f32[16,28,128,128]{3,1,2,0:T(8,128)} fusion(bf16[192,128,128]{2,1,0:T(8,128)(2,1)} %bitcast.112, s32[192]{0:T(256)S(1)} %bitcast.119, s32[16,28]{1,0:T(8,128)S(1)} %multiply_add_fusion.1), kind=kOutput, calls=%fused_computation.39 | convolution fusion | flops 2818658304 | bytes 35654144 | tf_op jit(solution)/shard_map/sk,sij->kij/dot_general | solution.py:25
  95.8 34.6 %copy.176 = f32[256,8,28,128]{3,1,2,0:T(8,128)} copy(f32[256,8,28,128]{3,2,1,0:T(8,128)} %bitcast.101) | data formatting | bytes 58720256
  130.4 29.7 %copy.147 = f32[2048,3584]{0,1:T(8,128)} copy(f32[2048,3584]{1,0:T(8,128)} %bitcast.103) | data formatting | bytes 58720256 | tf_op jit(solution)/shard_map/reshape | solution.py:27
  160.1 34.7 %copy.175 = f32[256,8,28,128]{3,1,2,0:T(8,128)} copy(f32[256,8,28,128]{3,2,1,0:T(8,128)} %bitcast.102) | data formatting | bytes 58720256
  194.9 29.7 %copy.148 = f32[2048,3584]{0,1:T(8,128)} copy(f32[2048,3584]{1,0:T(8,128)} %bitcast.104) | data formatting | bytes 58720256 | tf_op jit(solution)/shard_map/reshape | solution.py:27
  224.6 20.4 %copy.116 = bf16[2048,3584]{0,1:T(8,128)(2,1)} copy(bf16[2048,3584]{1,0:T(8,128)(2,1)} %param.17) | data formatting | bytes 29360128 | tf_op args[2]
  245.0 20.4 %copy.119 = bf16[2048,3584]{0,1:T(8,128)(2,1)} copy(bf16[2048,3584]{1,0:T(8,128)(2,1)} %param.18) | data formatting | bytes 29360128 | tf_op args[3]
  265.3 39.0 %add_convert_fusion = (bf16[2048,3584]{0,1:T(8,128)(2,1)}, bf16[2048,3584]{0,1:T(8,128)(2,1)}) fusion(f32[2048,3584]{0,1:T(8,128)} %copy.148, bf16[2048,3584]{0,1:T(8,128)(2,1)} %copy.119, f32[2048,3584]{0,1:T(8,128)} %copy.147, bf16[2048,3584]{0,1:T(8,128)(2,1)} %copy.116), kind=kLoop, calls=%fused_computation.11 | loop fusion | flops 44040192 | bytes 117440512 | tf_op jit(solution)/shard_map/convert_element_type | solution.py:28
  304.4 15.9 %fusion.24 = f32[256,7168]{0,1:T(8,128)} fusion(bf16[256,2048]{1,0:T(8,128)(2,1)} %all-gather.4.cloned.1.call-done, bf16[2048,3584]{0,1:T(8,128)(2,1)} %get-tuple-element.33, bf16[2048,3584]{0,1:T(8,128)(2,1)} %get-tuple-element.34), kind=kOutput, calls=%fused_computation.36 | convolution fusion | flops 7574913024 | bytes 37748736 | tf_op jit(solution)/shard_map/dot_general | solution.py:82
  320.3 8.4 %copy.149 = f32[256,7168]{1,0:T(8,128)} copy(f32[256,7168]{0,1:T(8,128)} %fusion.24) | data formatting | bytes 14680064
  328.8 129.6 %reduce-scatter.22.cloned.1.call-done = f32[64,7168]{1,0:T(8,128)} async-done(((f32[256,7168]{1,0:T(8,128)}), f32[64,7168]{1,0:T(8,128)}) %reduce-scatter.22.cloned.1.call-update) | async-done | bytes 1835024 | tf_op jit(solution)/shard_map/reduce_scatter | solution.py:81
  461.9 12.0 %collective-permute-done = bf16[64,3584]{1,0:T(8,128)(2,1)S(1)} collective-permute-done((bf16[64,3584]{1,0:T(8,128)(2,1)S(1)}, bf16[64,3584]{1,0:T(8,128)(2,1)S(1)}, u32[]{:S(2)}, u32[]{:S(2)}) %collective-permute-start) | collective-permute-done | bytes 458784 | tf_op jit(solution)/shard_map/ppermute | solution.py:11
  473.8 12.3 %collective-permute-done.1 = bf16[64,3584]{1,0:T(8,128)(2,1)S(1)} collective-permute-done((bf16[64,3584]{1,0:T(8,128)(2,1)S(1)}, bf16[64,3584]{1,0:T(8,128)(2,1)S(1)}, u32[]{:S(2)}, u32[]{:S(2)}) %collective-permute-start.1) | collective-permute-done | bytes 458784 | tf_op jit(solution)/shard_map/ppermute | solution.py:11
  487.2 10.4 %collective-permute-done.2 = bf16[64,3584]{1,0:T(8,128)(2,1)S(1)} collective-permute-done((bf16[64,3584]{1,0:T(8,128)(2,1)S(1)}, bf16[64,3584]{1,0:T(8,128)(2,1)S(1)}, u32[]{:S(2)}, u32[]{:S(2)}) %collective-permute-start.2) | collective-permute-done | bytes 458784 | tf_op jit(solution)/shard_map/ppermute | solution.py:11
  498.0 22.0 %fusion.67 = f32[256,2048]{1,0:T(8,128)} fusion(bf16[256,3584]{1,0:T(8,128)(2,1)S(1)} %constant_dynamic-slice_fusion, f32[448,8,16,128]{3,2,1,0:T(8,128)} %bitcast.100, bf16[3584,2048]{1,0:T(8,128)(2,1)} %param.19), kind=kOutput, calls=%fused_computation.120 | convolution fusion | flops 3780116480 | bytes 47972352 | tf_op jit(solution)/shard_map/dot_general | solution.py:93
  520.1 42.3 %all-gather.8.cloned.1.call-done = bf16[256,7168]{1,0:T(8,128)(2,1)} async-done(((bf16[64,7168]{1,0:T(8,128)(2,1)}), bf16[256,7168]{1,0:T(8,128)(2,1)}) %all-gather.8.cloned.1.call-update) | async-done | bytes 3670032 | tf_op jit(solution)/shard_map/all_gather | solution.py:107
  562.4 15.3 %fusion.1 = f32[256,2048]{1,0:T(8,128)} fusion(bf16[256,7168]{1,0:T(8,128)(2,1)} %all-gather.8.cloned.1.call-done, bf16[2048,3584]{0,1:T(8,128)(2,1)} %get-tuple-element.33, bf16[2048,3584]{0,1:T(8,128)(2,1)} %get-tuple-element.34), kind=kOutput, calls=%fused_computation.13 | convolution fusion | flops 7574913024 | bytes 35127296 | tf_op jit(solution)/shard_map/dot_general | solution.py:52
  581.2 8.2 %gather_fusion.5 = bf16[192,256,128]{2,1,0:T(8,128)(2,1)} fusion(bf16[256,16,128]{2,0,1:T(8,128)(2,1)S(1)} %copy.139, s32[1024]{0:T(1024)S(1)} %get-tuple-element.37), kind=kCustom, calls=%fused_computation.3.clone | custom fusion | bytes 25166592 | tf_op jit(solution)/shard_map/jit(_take)/gather | solution.py:42
  594.5 8.3 %gather_fusion.4 = bf16[192,256,128]{2,1,0:T(8,128)(2,1)} fusion(bf16[256,28,128]{2,0,1:T(8,128)(2,1)S(1)} %copy.137, s32[1024]{0:T(1024)S(1)} %get-tuple-element.38), kind=kCustom, calls=%fused_computation.5.clone | custom fusion | bytes 25166592 | tf_op jit(solution)/shard_map/jit(_take)/gather | solution.py:37
  602.8 14.2 %broadcast_multiply_fusion = f32[192,128,128]{2,1,0:T(8,128)} fusion(f32[192]{0:T(256)S(1)} %get-tuple-element.26, bf16[192,256,128]{2,1,0:T(8,128)(2,1)} %gather_fusion.5, pred[192]{0:T(512)(128)(4,1)S(1)} %get-tuple-element.24, bf16[192,256,128]{2,1,0:T(8,128)(2,1)} %gather_fusion.4, pred[192]{0:T(512)(128)(4,1)S(1)} %get-tuple-element.7), kind=kOutput, calls=%fused_computation.49 | convolution fusion | flops 1626341376 | bytes 37749888 | tf_op jit(solution)/shard_map/tsi,tsj->sij/dot_general | solution.py:47
  619.7 8.0 %gather_fusion = bf16[192,256,128]{2,1,0:T(8,128)(2,1)} fusion(bf16[256,16,128]{2,0,1:T(8,128)(2,1)S(1)} %copy.128, s32[1024]{0:T(1024)S(1)} %get-tuple-element.36), kind=kCustom, calls=%fused_computation.clone | custom fusion | bytes 25166592 | tf_op jit(solution)/shard_map/jit(_take)/gather | solution.py:37
  627.7 3.9 fusion.69
  636.7 7.9 %gather_fusion.1 = bf16[192,256,128]{2,1,0:T(8,128)(2,1)} fusion(bf16[256,28,128]{2,0,1:T(8,128)(2,1)S(1)} %copy.130, s32[1024]{0:T(1024)S(1)} %get-tuple-element.35), kind=kCustom, calls=%fused_computation.1.clone | custom fusion | bytes 25166592 | tf_op jit(solution)/shard_map/jit(_take)/gather | solution.py:42
  644.6 20.4 %broadcast_multiply_fusion.2 = f32[192,128,128]{2,1,0:T(8,128)} fusion(f32[192]{0:T(256)S(1)} %get-tuple-element.32, bf16[192,256,128]{2,1,0:T(8,128)(2,1)} %gather_fusion.1, pred[192]{0:T(512)(128)(4,1)S(1)} %get-tuple-element.30, bf16[192,256,128]{2,1,0:T(8,128)(2,1)} %gather_fusion, pred[192]{0:T(512)(128)(4,1)S(1)} %get-tuple-element.15), kind=kOutput, calls=%fused_computation.51 | convolution fusion | flops 1626341376 | bytes 37749888 | tf_op jit(solution)/shard_map/tsi,tsj->sij/dot_general | solution.py:47
  665.7 8.5 %gather_fusion.2 = bf16[192,256,128]{2,1,0:T(8,128)(2,1)} fusion(bf16[256,16,128]{2,0,1:T(8,128)(2,1)S(1)} %copy.128, s32[1024]{0:T(1024)S(1)} %get-tuple-element.40), kind=kCustom, calls=%fused_computation.2.clone | custom fusion | bytes 25166592 | tf_op jit(solution)/shard_map/jit(_take)/gather | solution.py:37
  679.7 8.8 %gather_fusion.3 = bf16[192,256,128]{2,1,0:T(8,128)(2,1)} fusion(bf16[256,28,128]{2,0,1:T(8,128)(2,1)S(1)} %copy.134, s32[1024]{0:T(1024)S(1)} %get-tuple-element.39), kind=kCustom, calls=%fused_computation.4.clone | custom fusion | bytes 25166592 | tf_op jit(solution)/shard_map/jit(_take)/gather | solution.py:42
  688.5 14.0 %broadcast_multiply_fusion.1 = f32[192,128,128]{2,1,0:T(8,128)} fusion(f32[192]{0:T(256)S(1)} %get-tuple-element.29, bf16[192,256,128]{2,1,0:T(8,128)(2,1)} %gather_fusion.3, pred[192]{0:T(512)(128)(4,1)S(1)} %get-tuple-element.27, bf16[192,256,128]{2,1,0:T(8,128)(2,1)} %gather_fusion.2, pred[192]{0:T(512)(128)(4,1)S(1)} %get-tuple-element.11), kind=kOutput, calls=%fused_computation.50 | convolution fusion | flops 1626341376 | bytes 37749888 | tf_op jit(solution)/shard_map/tsi,tsj->sij/dot_general | solution.py:47
  706.1 17.6 %reduce-scatter.18.cloned.1.call-done = f32[96,128,128]{2,1,0:T(8,128)} async-done(((f32[192,128,128]{2,1,0:T(8,128)}), f32[96,128,128]{2,1,0:T(8,128)}) %reduce-scatter.18.cloned.1.call-update) | async-done | bytes 6291472 | tf_op jit(solution)/shard_map/reduce_scatter | solution.py:121
  (82 shorter events, 32.7 us)
Async XLA Ops:
  7.2 39.6 %all-gather.6.cloned.1.call-start = ((), (), s32[]{:S(2)}) async-start(), calls=%async_computation.9 | async-start | bytes 1310720 | tf_op jit(solution)/shard_map/all_gather | solution.py:78
  7.2 20.2 %slice-start = ((s8[6291456]{0:T(1024)(128)(4,1)}), s8[2097152]{0:T(1024)(128)(4,1)S(1)}, s32[]{:S(2)}) async-start(s8[6291456]{0:T(1024)(128)(4,1)} %bitcast.109), calls=%async_computation.17 | async-start | bytes 4194304
  7.9 296.5 %all-gather.4.cloned.1.call-start = ((), (), s32[]{:S(2)}) async-start(), calls=%async_computation.7 | async-start | bytes 1310720 | tf_op jit(solution)/shard_map/all_gather | solution.py:77
  8.6 320.1 %reduce-scatter.24.cloned.1.call-start = ((), (), s32[]{:S(2)}) async-start(), calls=%async_computation.16 | async-start | bytes 4587520 | tf_op jit(solution)/shard_map/reduce_scatter | solution.py:99
  8.7 18.7 %slice-start.1 = ((s8[6291456]{0:T(1024)(128)(4,1)}), s8[4194304]{0:T(1024)(128)(4,1)S(1)}, s32[]{:S(2)}) async-start(s8[6291456]{0:T(1024)(128)(4,1)} %bitcast.109), calls=%async_computation.18 | async-start | bytes 8388608
  8.7 18.7 %copy-start.3 = (s32[1,1,192]{2,1,0:T(1,128)S(1)}, s32[1,1,192]{2,1,0:T(1,128)}, u32[]{:S(2)}) copy-start(s32[1,1,192]{2,1,0:T(1,128)} %param.25) | copy-start | bytes 2308
  46.7 30.0 %copy-start.6 = (s32[1,1,192]{2,1,0:T(1,128)S(1)}, s32[1,1,192]{2,1,0:T(1,128)}, u32[]{:S(2)}) copy-start(s32[1,1,192]{2,1,0:T(1,128)} %param.24) | copy-start | bytes 2308
  76.7 381.7 %reduce-scatter.22.cloned.1.call-start = ((), (), s32[]{:S(2)}) async-start(), calls=%async_computation.15 | async-start | bytes 9175040 | tf_op jit(solution)/shard_map/reduce_scatter | solution.py:81
  328.7 233.6 %all-gather.8.cloned.1.call-start = ((), (), s32[]{:S(2)}) async-start(), calls=%async_computation.10 | async-start | bytes 4587520 | tf_op jit(solution)/shard_map/all_gather | solution.py:107
  460.7 13.2 %collective-permute-start = (bf16[64,3584]{1,0:T(8,128)(2,1)S(1)}, bf16[64,3584]{1,0:T(8,128)(2,1)S(1)}, u32[]{:S(2)}, u32[]{:S(2)}) collective-permute-start(bf16[64,3584]{1,0:T(8,128)(2,1)S(1)} %get-tuple-element.23), channel_id=1, source_target_pairs={{0,2},{2,4},{4,6},{6,0},{1,3},{3,5},{5,7},{7,1},{8,10},{10,12},{12... | collective-permute-start | bytes 1376264 | tf_op jit(solution)/shard_map/ppermute | solution.py:11
  473.8 12.3 %collective-permute-start.1 = (bf16[64,3584]{1,0:T(8,128)(2,1)S(1)}, bf16[64,3584]{1,0:T(8,128)(2,1)S(1)}, u32[]{:S(2)}, u32[]{:S(2)}) collective-permute-start(bf16[64,3584]{1,0:T(8,128)(2,1)S(1)} %collective-permute-done), channel_id=1, source_target_pairs={{0,2},{2,4},{4,6},{6,0},{1,3},{3,5},{5,7},{7,1},{8,10},{10,12},{12... | collective-permute-start | bytes 1376264 | tf_op jit(solution)/shard_map/ppermute | solution.py:11
  486.1 11.4 %collective-permute-start.2 = (bf16[64,3584]{1,0:T(8,128)(2,1)S(1)}, bf16[64,3584]{1,0:T(8,128)(2,1)S(1)}, u32[]{:S(2)}, u32[]{:S(2)}) collective-permute-start(bf16[64,3584]{1,0:T(8,128)(2,1)S(1)} %collective-permute-done.1), channel_id=1, source_target_pairs={{0,2},{2,4},{4,6},{6,0},{1,3},{3,5},{5,7},{7,1},{8,10},{10,12},{12... | collective-permute-start | bytes 1376264 | tf_op jit(solution)/shard_map/ppermute | solution.py:11
  487.1 215.4 %reduce-scatter.12.cloned.1.call-start = ((), (), s32[]{:S(2)}) async-start(), calls=%async_computation.8 | async-start | bytes 2621440 | tf_op jit(solution)/shard_map/reduce_scatter | solution.py:92
  520.0 57.7 %copy-start.4 = (s32[1,1,192]{2,1,0:T(1,128)S(1)}, s32[1,1,192]{2,1,0:T(1,128)}, u32[]{:S(2)}) copy-start(s32[1,1,192]{2,1,0:T(1,128)} %param.25) | copy-start | bytes 2308
  520.0 57.7 %copy-start.1 = (bf16[256,2048]{1,0:T(8,128)(2,1)S(1)}, bf16[256,2048]{1,0:T(8,128)(2,1)}, u32[]{:S(2)}) copy-start(bf16[256,2048]{1,0:T(8,128)(2,1)} %all-gather.6.cloned.1.call-done) | copy-start | bytes 3145732
  520.0 184.2 %reduce-scatter.14.cloned.1.call-start = ((), (), s32[]{:S(2)}) async-start(), calls=%async_computation.11 | async-start | bytes 2621440 | tf_op jit(solution)/shard_map/reduce_scatter | solution.py:111
  577.7 128.4 %reduce-scatter.20.cloned.1.call-start = ((), (), s32[]{:S(2)}) async-start(), calls=%async_computation.14 | async-start | bytes 18874368 | tf_op jit(solution)/shard_map/reduce_scatter | solution.py:122
  617.0 0.7 copy-start.5
  617.0 1.3 copy-start.2
  617.1 89.0 %reduce-scatter.16.cloned.1.call-start = ((), (), s32[]{:S(2)}) async-start(), calls=%async_computation.12 | async-start | bytes 18874368 | tf_op jit(solution)/shard_map/reduce_scatter | solution.py:120
  665.0 0.7 copy-start.7
  665.0 58.7 %reduce-scatter.18.cloned.1.call-start = ((), (), s32[]{:S(2)}) async-start(), calls=%async_computation.13 | async-start | bytes 18874368 | tf_op jit(solution)/shard_map/reduce_scatter | solution.py:121
  665.7 8.5 %copy-start = (bf16[256,3584]{1,0:T(8,128)(2,1)S(1)}, bf16[256,3584]{1,0:T(8,128)(2,1)}, u32[]{:S(2)}) copy-start(bf16[256,3584]{1,0:T(8,128)(2,1)} %get-tuple-element.19) | copy-start | bytes 5505028
Sparse Core Ops, SparseCore 0:
  9.8 28.3 all-gather.5
  40.1 26.4 all-gather.3
  76.8 70.0 reduce-scatter.23
  328.8 129.5 reduce-scatter.21
  487.3 75.0 all-gather.7
  565.2 33.7 reduce-scatter.11
  601.9 35.1 reduce-scatter.13
  640.0 22.6 reduce-scatter.19
  665.6 22.9 reduce-scatter.15
  702.6 21.0 reduce-scatter.17
